TPU v7x, 256 devices: a whole 4x4x8 slice. The times are simulated.
256 devices in a mesh: dp: 16 (over y, x), expert: 16 (over z, core).
Axes of the slice: x: 4, y: 4, z: 8, core: 2. Of those that a mesh axis runs over, the one named last changes fastest.
Arguments:
- tokens: bfloat16 [16384, 2048], P(('dp', 'expert')), may hold values from -6 to 6
- expert_ids: int32 [16384, 8], P(('dp', 'expert')), may hold values from 0 to 31, all different within a row; in each aligned block of 64 rows (0 to 63, 64 to 127, ...) at most 24 rows name the same one
- gate_fixed: int32 [16384, 8], P(('dp', 'expert')), may hold values from 1 to 65535
- scorer_id: int32 [1024], P(('dp', 'expert')), may hold values from 0 to 1
- direction_tags: bfloat16 [2, 2048], replicated, may hold values from -6 to 6
- w_gate: bfloat16 [32, 2048, 512], P('expert'), may hold values from -0.125 to 0.125
- w_up: bfloat16 [32, 2048, 512], P('expert'), may hold values from -0.125 to 0.125
- w_down: bfloat16 [32, 512, 2048], P('expert'), may hold values from -0.25 to 0.25
- score_head: float32 [2048], replicated, may hold values from -0.125 to 0.125
Outputs:
- mixed: bfloat16 [16384, 2048], P(('dp', 'expert'))
- pair_score: float32 [1024], P(('dp', 'expert'))
Inputs may be any that keep to these rules, and one draw needn't show every extreme that they name: `expert_ids`: each row names 8 different experts. Among the rows of one device no expert is named by more than 24 rows, and in some devices' rows an expert is named by exactly 24.
All inputs are finite; a program needn't handle non-finite values.
Results may differ from a plain program's by a relative error of at most 0.04.
Values may be sent and summed in bfloat16 or wider, within the bound.
A program may use at most 64 MiB of HBM per device.

v0:
```python
import jax
import jax.numpy as jnp
from jax import lax
from jax.sharding import PartitionSpec as P

SEQ_LEN = 16
MOST = 24


def from_partner(block, axis, bit):
    count = lax.axis_size(axis)
    route = []
    for low in range(count):
        high = low | 1 << bit
        if high != low and high < count:
            route += [(low, high), (high, low)]
    return lax.ppermute(block, axis, route)


def route_ranks(expert_ids, expert_total):
    flat_ids = expert_ids.reshape(-1)
    entry_count = flat_ids.shape[0]
    onehot = flat_ids[:, None] == jnp.arange(expert_total, dtype=jnp.int32)[None, :]
    positions = jnp.arange(entry_count, dtype=jnp.int32)
    earlier = (positions[:, None] > positions[None, :]).astype(jnp.bfloat16)
    counts = jnp.dot(earlier, onehot.astype(jnp.bfloat16), preferred_element_type=jnp.float32)
    rank_in = jnp.sum(jnp.where(onehot, counts, 0.0), axis=1).astype(jnp.int32)
    return rank_in.reshape(expert_ids.shape)


def body(
    tokens, expert_ids, gate_fixed, scorer_id, direction_tags, w_gate, w_up, w_down, score_head
):
    expert_count = lax.axis_size("expert")
    per_device = w_gate.shape[0]
    tok_rows, model_width = tokens.shape
    top_count = expert_ids.shape[1]
    which_tag = jnp.repeat(scorer_id, SEQ_LEN)[:, None]
    tag_rows = jnp.where(
        which_tag == 1, direction_tags[1][None, :], direction_tags[0][None, :]
    ).astype(jnp.float32)
    inputs = (tokens.astype(jnp.float32) + tag_rows).astype(jnp.bfloat16)
    fixed_val = gate_fixed.astype(jnp.float32)
    weight = fixed_val / jnp.sum(fixed_val, axis=1, keepdims=True)
    rank_in = route_ranks(expert_ids, per_device * expert_count)
    inputs_all, ids_all, weight_all, rank_all = (
        lax.all_gather(inputs, "expert", axis=0, tiled=True),
        lax.all_gather(expert_ids, "expert", axis=0, tiled=True),
        lax.all_gather(weight.astype(jnp.bfloat16), "expert", axis=0, tiled=True).astype(
            weight.dtype
        ),
        lax.all_gather(rank_in, "expert", axis=0, tiled=True),
    )
    my_index = lax.axis_index("expert")
    local_count = per_device * MOST
    ids_cube = ids_all.reshape(expert_count, tok_rows, top_count)
    rank_cube = rank_all.reshape(expert_count, tok_rows, top_count)
    weight_cube = weight_all.reshape(expert_count, tok_rows, top_count)
    local_slot = ids_cube - my_index * per_device
    is_mine = (local_slot >= 0) & (local_slot < per_device)
    local_key = jnp.where(is_mine, local_slot * MOST + rank_cube, -1)
    match = (
        local_key[:, None, :, :] == jnp.arange(local_count, dtype=jnp.int32)[None, :, None, None]
    )
    picker = jnp.any(match, axis=3).astype(jnp.bfloat16)
    slot_weight = jnp.sum(jnp.where(match, weight_cube[:, None, :, :], 0.0), axis=(2, 3)).reshape(
        expert_count, per_device, MOST
    )
    inputs_cube = inputs_all.reshape(expert_count, tok_rows, model_width)
    row_block = jnp.einsum(
        "sqt,std->sqd", picker, inputs_cube, preferred_element_type=jnp.float32
    ).astype(jnp.bfloat16)
    row_block = row_block.reshape(expert_count, per_device, MOST, model_width)
    gate_proj = jnp.einsum("nemd,edf->nemf", row_block, w_gate, preferred_element_type=jnp.float32)
    up_proj = jnp.einsum("nemd,edf->nemf", row_block, w_up, preferred_element_type=jnp.float32)
    hidden = (jax.nn.silu(gate_proj) * up_proj).astype(jnp.bfloat16)
    down_out = jnp.einsum("nemf,efd->nemd", hidden, w_down, preferred_element_type=jnp.float32)
    result = (slot_weight[..., None] * down_out).astype(jnp.bfloat16)
    partial_value = jnp.einsum(
        "sqt,sqd->std",
        picker,
        result.reshape(expert_count, local_count, model_width),
        preferred_element_type=jnp.float32,
    )
    partial_value = partial_value.reshape(expert_count * tok_rows, model_width)
    received = lax.all_to_all(
        partial_value.astype(jnp.bfloat16), "expert", split_axis=0, concat_axis=0, tiled=True
    ).astype(partial_value.dtype)
    summed = received.reshape(expert_count, tok_rows, model_width).sum(axis=0)
    mixed = summed.astype(jnp.bfloat16)
    token_score = jnp.dot(mixed.astype(jnp.float32), score_head, precision=lax.Precision.HIGHEST)
    seq_score = token_score.reshape(-1, SEQ_LEN).sum(axis=1)
    partner = from_partner(seq_score, "dp", lax.axis_size("dp").bit_length() - 2)
    pair_score = jnp.abs(seq_score - partner) + 0.5 * (seq_score + partner)
    return (mixed, pair_score)


def solution(mesh):
    return jax.shard_map(
        body,
        mesh=mesh,
        in_specs=(
            P(("dp", "expert"), None),
            P(("dp", "expert"), None),
            P(("dp", "expert"), None),
            P(("dp", "expert")),
            P(),
            P("expert", None, None),
            P("expert", None, None),
            P("expert", None, None),
            P(),
        ),
        out_specs=(P(("dp", "expert"), None), P(("dp", "expert"))),
        check_vma=False,
    )
```

profile of v0, /device:TPU:1, one launch (start us, length us, event | category | flops | bytes accessed | tf_op | source)
XLA Modules:
  0.0 203.0 jit_solution(7624634206513829561)
XLA Ops:
  7.2 0.0 all-gather.5.cloned.1.call-start
  7.2 0.7 broadcast_compare_fusion
  7.9 0.1 broadcast_in_dim.68
  8.0 0.1 eq.52
  8.1 0.8 slice_reduce_fusion.1
  8.9 1.8 add_convert_fusion
  10.7 0.7 convert_reduce_fusion
  11.4 0.7 fusion.27
  12.1 21.4 %all-gather.2 = bf16[16,64,8]{1,2,0:T(8,128)(2,1)S(1)} all-gather(bf16[1,64,8]{1,2,0:T(8,128)(2,1)S(1)} %fusion.27), channel_id=1, replica_groups=mesh['dp'=16,'expert'=16] {'expert'}, dimensions={0}, use_global_device_ids=true | all-gather | bytes 17408 | tf_op jit(solution)/shard_map/all_gather | solution.py:49
  33.5 0.8 copy.28
  34.2 0.1 eq.43
  34.3 0.3 fusion.20
  34.6 0.1 reshape.70
  34.7 0.1 copy.29
  34.8 14.6 %all-gather.1 = s32[16,64,8]{1,2,0:T(8,128)S(1)} all-gather(s32[1,64,8]{1,2,0:T(8,128)S(1)} %copy.29), channel_id=1, replica_groups=mesh['dp'=16,'expert'=16] {'expert'}, dimensions={0}, use_global_device_ids=true | all-gather | bytes 34816 | tf_op jit(solution)/shard_map/all_gather | solution.py:52
  49.4 16.2 %all-gather = s32[16,64,8]{1,2,0:T(8,128)S(1)} all-gather(s32[1,64,8]{1,2,0:T(8,128)} %bitcast.68), channel_id=1, replica_groups=mesh['dp'=16,'expert'=16] {'expert'}, dimensions={0}, use_global_device_ids=true | all-gather | bytes 34816 | tf_op jit(solution)/shard_map/all_gather | solution.py:48
  65.7 1.7 select_reduce_fusion
  67.3 0.1 mul.37
  67.4 1.2 fusion.9
  68.6 3.3 %convolution_convert_fusion.1 = bf16[16,48,2048]{2,1,0:T(8,128)(2,1)S(1)} fusion(pred[16,48,64]{2,1,0:T(8,128)(4,1)S(1)} %fusion.9, bf16[16,64,2048]{2,1,0:T(8,128)(2,1)} %bitcast.64), kind=kOutput, calls=%fused_computation.9 | convolution fusion | flops 202899456 | bytes 7389184 | tf_op jit(solution)/shard_map/sqt,std->sqd/dot_general | solution.py:70
  71.9 0.1 copy-done.2
  72.1 3.0 %fusion.5 = f32[2,16,24,512]{3,2,1,0:T(8,128)} fusion(bf16[2,2048,512]{2,1,0:T(8,128)(2,1)S(1)} %copy-done.2, bf16[16,2,24,2048]{3,2,1,0:T(8,128)(2,1)S(1)} %bitcast.65), kind=kOutput, calls=%fused_computation.6 | convolution fusion | flops 1610612736 | bytes 8912896 | tf_op jit(solution)/shard_map/nemd,edf->nemf/dot_general | solution.py:74
  75.0 9.2 %fusion = bf16[16,2,24,2048]{3,2,0,1:T(8,128)(2,1)} fusion(bf16[2,512,2048]{2,1,0:T(8,128)(2,1)} %param.16, f32[16,2,24]{2,0,1:T(8,128)S(1)} %copy.30, f32[2,16,24,512]{3,2,1,0:T(8,128)} %fusion.5, bf16[2,2048,512]{2,1,0:T(8,128)(2,1)} %param.15, bf16[16,2,24,2048]{3,2,1,0:T(8,128)(2,1)S(1)} %bitcast.66), kind=kOutput, calls=%fused_computation.1 | convolution fusion | flops 3226730496 | bytes 16256000 | tf_op jit(solution)/shard_map/nemf,efd->nemd/dot_general | solution.py:77
  84.2 2.3 %copy.33 = bf16[16,2,24,2048]{3,2,1,0:T(8,128)(2,1)S(1)} copy(bf16[16,2,24,2048]{3,2,0,1:T(8,128)(2,1)} %fusion) | data formatting | bytes 6291456 | tf_op jit(solution)/shard_map/convert_element_type | solution.py:78
  86.5 1.3 convolution_convert_fusion
  87.8 99.7 %all_to_all.6 = bf16[16,64,2048]{2,1,0:T(8,128)(2,1)} all-to-all(bf16[16,64,2048]{2,1,0:T(8,128)(2,1)S(1)} %convolution_convert_fusion), channel_id=1, replica_groups=mesh['dp'=16,'expert'=16] {'expert'}, dimensions={0} | all-to-all | bytes 8388608 | tf_op jit(solution)/shard_map/all_to_all | solution.py:86
  187.5 3.0 %reduce_sum.51 = bf16[64,2048]{1,0:T(8,128)(2,1)S(1)} reduce(bf16[16,64,2048]{2,1,0:T(8,128)(2,1)} %all_to_all.6, bf16[]{:T(256)} %constant.24.clone.1), dimensions={0}, to_apply=%region_4.5 | reduce | flops 1966080 | bytes 4456450 | tf_op jit(solution)/shard_map/reduce_sum | solution.py:89
  190.5 1.0 fusion.29
  191.5 0.1 reduce_sum.52
  191.6 3.0 %collective-permute-start = (f32[4]{0:T(128)S(1)}, f32[4]{0:T(128)S(1)}, u32[]{:S(2)}, u32[]{:S(2)}) collective-permute-start(f32[4]{0:T(128)S(1)} %reduce_sum.52), channel_id=1, source_target_pairs={{0,128},{128,0},{16,144},{144,16},{32,160},{160,32},{48,176},{176,... | collective-permute-start | bytes 56 | tf_op jit(solution)/shard_map/ppermute | solution.py:17
  194.6 1.0 collective-permute-done
  195.6 0.5 multiply_add_fusion
  (11 shorter events, 0.1 us)
Async XLA Ops:
  7.2 183.3 %copy-start = (f32[2048]{0:T(1024)S(1)}, f32[2048]{0:T(1024)}, u32[]{:S(2)}) copy-start(f32[2048]{0:T(1024)} %param.17) | copy-start | bytes 24580
  7.2 61.4 %all-gather.5.cloned.1.call-start = ((), (), s32[]{:S(2)}) async-start(), calls=%async_computation.1 | async-start | bytes 4456448 | tf_op jit(solution)/shard_map/all_gather | solution.py:47
  68.6 3.5 %copy-start.2 = (bf16[2,2048,512]{2,1,0:T(8,128)(2,1)S(1)}, bf16[2,2048,512]{2,1,0:T(8,128)(2,1)}, u32[]{:S(2)}) copy-start(bf16[2,2048,512]{2,1,0:T(8,128)(2,1)} %param.14) | copy-start | bytes 12582916
  190.5 5.7 %copy-start.1 = (bf16[64,2048]{1,0:T(8,128)(2,1)}, bf16[64,2048]{1,0:T(8,128)(2,1)S(1)}, u32[]{:S(2)}) copy-start(bf16[64,2048]{1,0:T(8,128)(2,1)S(1)} %reduce_sum.51) | copy-start | bytes 786436
  191.6 4.0 %collective-permute-start = (f32[4]{0:T(128)S(1)}, f32[4]{0:T(128)S(1)}, u32[]{:S(2)}, u32[]{:S(2)}) collective-permute-start(f32[4]{0:T(128)S(1)} %reduce_sum.52), channel_id=1, source_target_pairs={{0,128},{128,0},{16,144},{144,16},{32,160},{160,32},{48,176},{176,... | collective-permute-start | bytes 56 | tf_op jit(solution)/shard_map/ppermute | solution.py:17
Sparse Core Ops, SparseCore 0:
  10.8 46.5 all-gather.4
where the time goes:
time: 203 us
  blocking collectives  152 us (75%)
  matrix products  18 us (9%)
  between operations  14.2 us (7%)
  other arithmetic  10.3 us (5%)
  local copies, waits for them, and re-layouts  4.53 us (2%)
  starting transfers between devices  3.04 us (1%)
    all_to_all x1, blocking collectives, body(): lax.all_to_all(partial_value.astype(jnp.bfloat16), 'expert', split_axis=0...  99.7 us
    all_gather x1, blocking collectives, body(): lax.all_gather(weight.astype(jnp.bfloat16), 'expert', axis=0, tiled=True)  21.4 us
    all_gather x1, blocking collectives, body(): lax.all_gather(expert_ids, 'expert', axis=0, tiled=True)  16.2 us
    all_gather x1, blocking collectives, body(): lax.all_gather(rank_in, 'expert', axis=0, tiled=True)  14.6 us
    dot_general x1, matrix products, body(): jnp.einsum('nemf,efd->nemd', hidden, w_down, preferred_element_type=jnp.f...  9.16 us
  transfers between devices with their start and end apart: 2, of which 1 were waited for; matrix products, arithmetic and copies ran while one was open for 3% of the time, Pallas kernels for 0%

commit v1 on v0

--- a/solution.py
+++ b/solution.py
@@ -5,6 +5,28 @@
 
 SEQ_LEN = 16
 MOST = 24
+
+
+def joined_along(tiles, dim):
+    tiles = jnp.moveaxis(tiles, 0, dim)
+    dims = tiles.shape
+    return tiles.reshape(*dims[:dim], dims[dim] * dims[dim + 1], *dims[dim + 2 :])
+
+
+def gather_around(x, axis, dim):
+    size = lax.axis_size(axis)
+    pairs = [(i, (i + 1) % size) for i in range(size)]
+    back = [(b, a) for a, b in pairs]
+    lower, upper = ([], [])
+    for step in range(size - 1):
+        if step % 2 == 0:
+            lower.append(lax.ppermute(lower[-1] if lower else x, axis, pairs))
+        else:
+            upper.append(lax.ppermute(upper[-1] if upper else x, axis, back))
+    parts = jnp.stack([*lower[::-1], x, *upper])
+    shift = lax.axis_index(axis) - len(lower)
+    parts = parts[(jnp.arange(size) - shift) % size]
+    return joined_along(parts, dim)
 
 
 def from_partner(block, axis, bit):
@@ -45,7 +67,7 @@
     rank_in = route_ranks(expert_ids, per_device * expert_count)
     inputs_all, ids_all, weight_all, rank_all = (
         lax.all_gather(inputs, "expert", axis=0, tiled=True),
-        lax.all_gather(expert_ids, "expert", axis=0, tiled=True),
+        gather_around(expert_ids, "expert", 0),
         lax.all_gather(weight.astype(jnp.bfloat16), "expert", axis=0, tiled=True).astype(
             weight.dtype
         ),

time: 203 us -> 217 us (1.069)
  starting transfers between devices: 3.04 us -> 25 us
  blocking collectives: 152 us -> 135 us
  waiting for transfers between devices: 1.02 us -> 8.1 us
    ppermute x0 -> x15, starting transfers between devices: none -> 22.1 us  [the longest x7 15.2 us: gather_around(): upper.append(lax.ppermute(upper[-1] if upper else x, axis, back))]
    all_gather x1 -> x0, blocking collectives: 16.2 us -> none  [body(): lax.all_gather(expert_ids, 'expert', axis=0, tiled=True)]
    ppermute x0 -> x15, waiting for transfers between devices: none -> 6.91 us  [the longest x7 4.06 us: gather_around(): upper.append(lax.ppermute(upper[-1] if upper else x, axis, back))]
    all_gather x1, blocking collectives: 21.4 us -> 15.8 us  [body(): lax.all_gather(weight.astype(jnp.bfloat16), 'expert', axis=0, tiled=True)]
    all_gather x1, blocking collectives: 14.6 us -> 17.9 us  [body(): lax.all_gather(rank_in, 'expert', axis=0, tiled=True)]
  transfers between devices with their start and end apart: 2 -> 17, of which waited for: 1 -> 7; matrix products, arithmetic and copies ran while one was open for 3% -> 3% of each run, Pallas kernels for 0% -> 0%
where the time goes in v1:
time: 217 us; the launch traced here: 216 us
  blocking collectives  135 us (62%)
  starting transfers between devices  25 us (12%)
  matrix products  18 us (8%)
  between operations  14.3 us (7%)
  other arithmetic  10.3 us (5%)
  waiting for transfers between devices  8.1 us (4%)
  local copies, waits for them, and re-layouts  5.82 us (3%)
    all_to_all x1, blocking collectives, body(): lax.all_to_all(partial_value.astype(jnp.bfloat16), 'expert', split_axis=0...  101 us
    all_gather x1, blocking collectives, body(): lax.all_gather(rank_in, 'expert', axis=0, tiled=True)  17.9 us
    all_gather x1, blocking collectives, body(): lax.all_gather(weight.astype(jnp.bfloat16), 'expert', axis=0, tiled=True)  15.8 us
    ppermute x7, starting transfers between devices, gather_around(): upper.append(lax.ppermute(upper[-1] if upper else x, axis, back))  15.2 us
    dot_general x1, matrix products, body(): jnp.einsum('nemf,efd->nemd', hidden, w_down, preferred_element_type=jnp.f...  9.16 us
    ppermute x8, starting transfers between devices, gather_around(): lower.append(lax.ppermute(lower[-1] if lower else x, axis, pairs))  6.95 us
  transfers between devices with their start and end apart: 17, of which 7 were waited for; matrix products, arithmetic and copies ran while one was open for 3% of the time, Pallas kernels for 0%

profile of v1, /device:TPU:1, one launch (start us, length us, event | category | flops | bytes accessed | tf_op | source)
XLA Modules:
  0.0 216.2 jit_solution(3198029366911812746)
XLA Ops:
  7.2 0.7 broadcast_compare_fusion
  8.1 0.8 slice_reduce_fusion.1
  8.9 1.8 add_convert_fusion
  10.7 3.0 %collective-permute-start = (s32[64,8]{0,1:T(8,128)}, s32[64,8]{0,1:T(8,128)S(1)}, u32[]{:S(2)}, u32[]{:S(2)}) collective-permute-start(s32[64,8]{0,1:T(8,128)} %param.10), channel_id=1, source_target_pairs={{0,1},{1,2},{2,3},{3,4},{4,5},{5,6},{6,7},{7,8},{8,9},{9,10},{10,1... | collective-permute-start | bytes 6152 | tf_op jit(solution)/shard_map/ppermute | solution.py:23
  14.0 0.8 collective-permute-done
  14.8 2.2 collective-permute-start.1
  17.0 0.7 convert_reduce_fusion
  17.7 2.0 collective-permute-done.1
  20.0 0.7 fusion.27
  20.7 0.8 copy.35
  21.6 3.3 %collective-permute-start.9 = (s32[64,8]{0,1:T(8,128)S(1)}, s32[64,8]{0,1:T(8,128)S(1)}, u32[]{:S(2)}, u32[]{:S(2)}) collective-permute-start(s32[64,8]{0,1:T(8,128)S(1)} %collective-permute-done.8), channel_id=1, source_target_pairs={{1,0},{2,1},{3,2},{4,3},{5,4},{6,5},{7,6},{8,7},{9,8},{10,9},{11,1... | collective-permute-start | bytes 6152 | tf_op jit(solution)/shard_map/ppermute | solution.py:25
  25.7 3.5 %collective-permute-start.10 = (s32[64,8]{0,1:T(8,128)S(1)}, s32[64,8]{0,1:T(8,128)S(1)}, u32[]{:S(2)}, u32[]{:S(2)}) collective-permute-start(s32[64,8]{0,1:T(8,128)S(1)} %collective-permute-done.9), channel_id=1, source_target_pairs={{1,0},{2,1},{3,2},{4,3},{5,4},{6,5},{7,6},{8,7},{9,8},{10,9},{11,1... | collective-permute-start | bytes 6152 | tf_op jit(solution)/shard_map/ppermute | solution.py:25
  29.1 0.8 collective-permute-done.10
  29.9 3.9 %collective-permute-start.11 = (s32[64,8]{0,1:T(8,128)S(1)}, s32[64,8]{0,1:T(8,128)S(1)}, u32[]{:S(2)}, u32[]{:S(2)}) collective-permute-start(s32[64,8]{0,1:T(8,128)S(1)} %collective-permute-done.10), channel_id=1, source_target_pairs={{1,0},{2,1},{3,2},{4,3},{5,4},{6,5},{7,6},{8,7},{9,8},{10,9},{11,1... | collective-permute-start | bytes 6152 | tf_op jit(solution)/shard_map/ppermute | solution.py:25
  34.6 3.8 %collective-permute-start.12 = (s32[64,8]{0,1:T(8,128)S(1)}, s32[64,8]{0,1:T(8,128)S(1)}, u32[]{:S(2)}, u32[]{:S(2)}) collective-permute-start(s32[64,8]{0,1:T(8,128)S(1)} %collective-permute-done.11), channel_id=1, source_target_pairs={{1,0},{2,1},{3,2},{4,3},{5,4},{6,5},{7,6},{8,7},{9,8},{10,9},{11,1... | collective-permute-start | bytes 6152 | tf_op jit(solution)/shard_map/ppermute | solution.py:25
  38.4 17.9 %all-gather = s32[16,64,8]{1,2,0:T(8,128)S(1)} all-gather(s32[1,64,8]{1,2,0:T(8,128)S(1)} %copy.36), channel_id=1, replica_groups=mesh['dp'=16,'expert'=16] {'expert'}, dimensions={0}, use_global_device_ids=true | all-gather | bytes 34816 | tf_op jit(solution)/shard_map/all_gather | solution.py:74
  56.7 1.4 collective-permute-start.7
  58.1 15.8 %all-gather.1 = bf16[16,64,8]{1,2,0:T(8,128)(2,1)S(1)} all-gather(bf16[1,64,8]{1,2,0:T(8,128)(2,1)S(1)} %fusion.27), channel_id=1, replica_groups=mesh['dp'=16,'expert'=16] {'expert'}, dimensions={0}, use_global_device_ids=true | all-gather | bytes 17408 | tf_op jit(solution)/shard_map/all_gather | solution.py:71
  74.2 0.7 constant_dynamic-update-slice_fusion.7
  74.9 2.1 collective-permute-done.14
  77.6 1.7 select_reduce_fusion
  79.3 1.2 fusion.9
  80.6 3.3 %convolution_convert_fusion.1 = bf16[16,48,2048]{2,1,0:T(8,128)(2,1)S(1)} fusion(pred[16,48,64]{2,1,0:T(8,128)(4,1)S(1)} %fusion.9, bf16[16,64,2048]{2,1,0:T(8,128)(2,1)} %bitcast.97), kind=kOutput, calls=%fused_computation.10 | convolution fusion | flops 202899456 | bytes 7389184 | tf_op jit(solution)/shard_map/sqt,std->sqd/dot_general | solution.py:92
  84.0 3.0 %fusion.5 = f32[2,16,24,512]{3,2,1,0:T(8,128)} fusion(bf16[2,2048,512]{2,1,0:T(8,128)(2,1)S(1)} %copy-done.2, bf16[16,2,24,2048]{3,2,1,0:T(8,128)(2,1)S(1)} %bitcast.98), kind=kOutput, calls=%fused_computation.7 | convolution fusion | flops 1610612736 | bytes 8912896 | tf_op jit(solution)/shard_map/nemd,edf->nemf/dot_general | solution.py:96
  86.9 9.2 %fusion = bf16[16,2,24,2048]{3,2,0,1:T(8,128)(2,1)} fusion(bf16[2,512,2048]{2,1,0:T(8,128)(2,1)} %param.16, f32[16,2,24]{2,0,1:T(8,128)S(1)} %copy.37, f32[2,16,24,512]{3,2,1,0:T(8,128)} %fusion.5, bf16[2,2048,512]{2,1,0:T(8,128)(2,1)} %param.15, bf16[16,2,24,2048]{3,2,1,0:T(8,128)(2,1)S(1)} %bitcast.99), kind=kOutput, calls=%fused_computation.2 | convolution fusion | flops 3226730496 | bytes 16256000 | tf_op jit(solution)/shard_map/nemf,efd->nemd/dot_general | solution.py:99
  96.1 2.3 %copy.40 = bf16[16,2,24,2048]{3,2,1,0:T(8,128)(2,1)S(1)} copy(bf16[16,2,24,2048]{3,2,0,1:T(8,128)(2,1)} %fusion) | data formatting | bytes 6291456 | tf_op jit(solution)/shard_map/convert_element_type | solution.py:100
  98.4 1.3 convolution_convert_fusion
  99.7 101.0 %all_to_all.6 = bf16[16,64,2048]{2,1,0:T(8,128)(2,1)} all-to-all(bf16[16,64,2048]{2,1,0:T(8,128)(2,1)S(1)} %convolution_convert_fusion), channel_id=1, replica_groups=mesh['dp'=16,'expert'=16] {'expert'}, dimensions={0} | all-to-all | bytes 8388608 | tf_op jit(solution)/shard_map/all_to_all | solution.py:108
  200.7 3.0 %reduce_sum.51 = bf16[64,2048]{1,0:T(8,128)(2,1)S(1)} reduce(bf16[16,64,2048]{2,1,0:T(8,128)(2,1)} %all_to_all.6, bf16[]{:T(256)} %constant.43.clone.1), dimensions={0}, to_apply=%region_4.5 | reduce | flops 1966080 | bytes 4456450 | tf_op jit(solution)/shard_map/reduce_sum | solution.py:111
  203.7 1.0 fusion.31
  204.8 2.8 %collective-permute-start.15 = (f32[4]{0:T(128)S(1)}, f32[4]{0:T(128)S(1)}, u32[]{:S(2)}, u32[]{:S(2)}) collective-permute-start(f32[4]{0:T(128)S(1)} %reduce_sum.52), channel_id=1, source_target_pairs={{0,128},{128,0},{16,144},{144,16},{32,160},{160,32},{48,176},{176,... | collective-permute-start | bytes 56 | tf_op jit(solution)/shard_map/ppermute | solution.py:39
  207.7 1.2 collective-permute-done.15
  (59 shorter events, 4.6 us)
Async XLA Ops:
  7.2 196.5 %copy-start = (f32[2048]{0:T(1024)S(1)}, f32[2048]{0:T(1024)}, u32[]{:S(2)}) copy-start(f32[2048]{0:T(1024)} %param.17) | copy-start | bytes 24580
  7.2 73.4 %all-gather.4.cloned.1.call-start = ((), (), s32[]{:S(2)}) async-start(), calls=%async_computation.1 | async-start | bytes 4456448 | tf_op jit(solution)/shard_map/all_gather | solution.py:69
  10.7 4.1 %collective-permute-start = (s32[64,8]{0,1:T(8,128)}, s32[64,8]{0,1:T(8,128)S(1)}, u32[]{:S(2)}, u32[]{:S(2)}) collective-permute-start(s32[64,8]{0,1:T(8,128)} %param.10), channel_id=1, source_target_pairs={{0,1},{1,2},{2,3},{3,4},{4,5},{5,6},{6,7},{7,8},{8,9},{9,10},{10,1... | collective-permute-start | bytes 6152 | tf_op jit(solution)/shard_map/ppermute | solution.py:23
  13.7 7.8 %collective-permute-start.8 = (s32[64,8]{0,1:T(8,128)}, s32[64,8]{0,1:T(8,128)S(1)}, u32[]{:S(2)}, u32[]{:S(2)}) collective-permute-start(s32[64,8]{0,1:T(8,128)} %param.10), channel_id=1, source_target_pairs={{1,0},{2,1},{3,2},{4,3},{5,4},{6,5},{7,6},{8,7},{9,8},{10,9},{11,1... | collective-permute-start | bytes 6152 | tf_op jit(solution)/shard_map/ppermute | solution.py:25
  14.8 4.8 %collective-permute-start.1 = (s32[64,8]{0,1:T(8,128)S(1)}, s32[64,8]{0,1:T(8,128)S(1)}, u32[]{:S(2)}, u32[]{:S(2)}) collective-permute-start(s32[64,8]{0,1:T(8,128)S(1)} %collective-permute-done), channel_id=1, source_target_pairs={{0,1},{1,2},{2,3},{3,4},{4,5},{5,6},{6,7},{7,8},{8,9},{9,10},{10,1... | collective-permute-start | bytes 6152 | tf_op jit(solution)/shard_map/ppermute | solution.py:23
  19.7 5.2 %collective-permute-start.2 = (s32[64,8]{0,1:T(8,128)S(1)}, s32[64,8]{0,1:T(8,128)S(1)}, u32[]{:S(2)}, u32[]{:S(2)}) collective-permute-start(s32[64,8]{0,1:T(8,128)S(1)} %collective-permute-done.1), channel_id=1, source_target_pairs={{0,1},{1,2},{2,3},{3,4},{4,5},{5,6},{6,7},{7,8},{8,9},{9,10},{10,1... | collective-permute-start | bytes 6152 | tf_op jit(solution)/shard_map/ppermute | solution.py:23
  21.6 4.1 %collective-permute-start.9 = (s32[64,8]{0,1:T(8,128)S(1)}, s32[64,8]{0,1:T(8,128)S(1)}, u32[]{:S(2)}, u32[]{:S(2)}) collective-permute-start(s32[64,8]{0,1:T(8,128)S(1)} %collective-permute-done.8), channel_id=1, source_target_pairs={{1,0},{2,1},{3,2},{4,3},{5,4},{6,5},{7,6},{8,7},{9,8},{10,9},{11,1... | collective-permute-start | bytes 6152 | tf_op jit(solution)/shard_map/ppermute | solution.py:25
  24.8 4.3 %collective-permute-start.3 = (s32[64,8]{0,1:T(8,128)S(1)}, s32[64,8]{0,1:T(8,128)S(1)}, u32[]{:S(2)}, u32[]{:S(2)}) collective-permute-start(s32[64,8]{0,1:T(8,128)S(1)} %collective-permute-done.2), channel_id=1, source_target_pairs={{0,1},{1,2},{2,3},{3,4},{4,5},{5,6},{6,7},{7,8},{8,9},{9,10},{10,1... | collective-permute-start | bytes 6152 | tf_op jit(solution)/shard_map/ppermute | solution.py:23
  25.7 4.3 %collective-permute-start.10 = (s32[64,8]{0,1:T(8,128)S(1)}, s32[64,8]{0,1:T(8,128)S(1)}, u32[]{:S(2)}, u32[]{:S(2)}) collective-permute-start(s32[64,8]{0,1:T(8,128)S(1)} %collective-permute-done.9), channel_id=1, source_target_pairs={{1,0},{2,1},{3,2},{4,3},{5,4},{6,5},{7,6},{8,7},{9,8},{10,9},{11,1... | collective-permute-start | bytes 6152 | tf_op jit(solution)/shard_map/ppermute | solution.py:25
  29.1 4.7 %collective-permute-start.4 = (s32[64,8]{0,1:T(8,128)S(1)}, s32[64,8]{0,1:T(8,128)S(1)}, u32[]{:S(2)}, u32[]{:S(2)}) collective-permute-start(s32[64,8]{0,1:T(8,128)S(1)} %collective-permute-done.3), channel_id=1, source_target_pairs={{0,1},{1,2},{2,3},{3,4},{4,5},{5,6},{6,7},{7,8},{8,9},{9,10},{10,1... | collective-permute-start | bytes 6152 | tf_op jit(solution)/shard_map/ppermute | solution.py:23
  29.9 4.7 %collective-permute-start.11 = (s32[64,8]{0,1:T(8,128)S(1)}, s32[64,8]{0,1:T(8,128)S(1)}, u32[]{:S(2)}, u32[]{:S(2)}) collective-permute-start(s32[64,8]{0,1:T(8,128)S(1)} %collective-permute-done.10), channel_id=1, source_target_pairs={{1,0},{2,1},{3,2},{4,3},{5,4},{6,5},{7,6},{8,7},{9,8},{10,9},{11,1... | collective-permute-start | bytes 6152 | tf_op jit(solution)/shard_map/ppermute | solution.py:25
  33.8 4.6 %collective-permute-start.5 = (s32[64,8]{0,1:T(8,128)S(1)}, s32[64,8]{0,1:T(8,128)S(1)}, u32[]{:S(2)}, u32[]{:S(2)}) collective-permute-start(s32[64,8]{0,1:T(8,128)S(1)} %collective-permute-done.4), channel_id=1, source_target_pairs={{0,1},{1,2},{2,3},{3,4},{4,5},{5,6},{6,7},{7,8},{8,9},{9,10},{10,1... | collective-permute-start | bytes 6152 | tf_op jit(solution)/shard_map/ppermute | solution.py:23
  34.6 21.7 %collective-permute-start.12 = (s32[64,8]{0,1:T(8,128)S(1)}, s32[64,8]{0,1:T(8,128)S(1)}, u32[]{:S(2)}, u32[]{:S(2)}) collective-permute-start(s32[64,8]{0,1:T(8,128)S(1)} %collective-permute-done.11), channel_id=1, source_target_pairs={{1,0},{2,1},{3,2},{4,3},{5,4},{6,5},{7,6},{8,7},{9,8},{10,9},{11,1... | collective-permute-start | bytes 6152 | tf_op jit(solution)/shard_map/ppermute | solution.py:25
  38.4 18.3 %collective-permute-start.6 = (s32[64,8]{0,1:T(8,128)S(1)}, s32[64,8]{0,1:T(8,128)S(1)}, u32[]{:S(2)}, u32[]{:S(2)}) collective-permute-start(s32[64,8]{0,1:T(8,128)S(1)} %collective-permute-done.5), channel_id=1, source_target_pairs={{0,1},{1,2},{2,3},{3,4},{4,5},{5,6},{6,7},{7,8},{8,9},{9,10},{10,1... | collective-permute-start | bytes 6152 | tf_op jit(solution)/shard_map/ppermute | solution.py:23
  56.4 17.6 %collective-permute-start.13 = (s32[64,8]{0,1:T(8,128)S(1)}, s32[64,8]{0,1:T(8,128)S(1)}, u32[]{:S(2)}, u32[]{:S(2)}) collective-permute-start(s32[64,8]{0,1:T(8,128)S(1)} %collective-permute-done.12), channel_id=1, source_target_pairs={{1,0},{2,1},{3,2},{4,3},{5,4},{6,5},{7,6},{8,7},{9,8},{10,9},{11,1... | collective-permute-start | bytes 6152 | tf_op jit(solution)/shard_map/ppermute | solution.py:25
  56.7 17.4 %collective-permute-start.7 = (s32[64,8]{0,1:T(8,128)S(1)}, s32[64,8]{0,1:T(8,128)S(1)}, u32[]{:S(2)}, u32[]{:S(2)}) collective-permute-start(s32[64,8]{0,1:T(8,128)S(1)} %collective-permute-done.6), channel_id=1, source_target_pairs={{0,1},{1,2},{2,3},{3,4},{4,5},{5,6},{6,7},{7,8},{8,9},{9,10},{10,1... | collective-permute-start | bytes 6152 | tf_op jit(solution)/shard_map/ppermute | solution.py:23
  73.9 3.0 %collective-permute-start.14 = (s32[64,8]{0,1:T(8,128)S(1)}, s32[64,8]{0,1:T(8,128)S(1)}, u32[]{:S(2)}, u32[]{:S(2)}) collective-permute-start(s32[64,8]{0,1:T(8,128)S(1)} %collective-permute-done.13), channel_id=1, source_target_pairs={{1,0},{2,1},{3,2},{4,3},{5,4},{6,5},{7,6},{8,7},{9,8},{10,9},{11,1... | collective-permute-start | bytes 6152 | tf_op jit(solution)/shard_map/ppermute | solution.py:25
  80.5 3.5 %copy-start.2 = (bf16[2,2048,512]{2,1,0:T(8,128)(2,1)S(1)}, bf16[2,2048,512]{2,1,0:T(8,128)(2,1)}, u32[]{:S(2)}) copy-start(bf16[2,2048,512]{2,1,0:T(8,128)(2,1)} %param.14) | copy-start | bytes 12582916
  203.7 5.7 %copy-start.1 = (bf16[64,2048]{1,0:T(8,128)(2,1)}, bf16[64,2048]{1,0:T(8,128)(2,1)S(1)}, u32[]{:S(2)}) copy-start(bf16[64,2048]{1,0:T(8,128)(2,1)S(1)} %reduce_sum.51) | copy-start | bytes 786436
  204.8 4.0 %collective-permute-start.15 = (f32[4]{0:T(128)S(1)}, f32[4]{0:T(128)S(1)}, u32[]{:S(2)}, u32[]{:S(2)}) collective-permute-start(f32[4]{0:T(128)S(1)} %reduce_sum.52), channel_id=1, source_target_pairs={{0,128},{128,0},{16,144},{144,16},{32,160},{160,32},{48,176},{176,... | collective-permute-start | bytes 56 | tf_op jit(solution)/shard_map/ppermute | solution.py:39
Sparse Core Ops, SparseCore 0:
  10.8 46.1 all-gather.3
